TPU v7x, 32 devices: a whole 2x2x4 slice. The times are simulated.
32 devices in a mesh: seg: 4 (over z), sec: 8 (over y, x, core).
Axes of the slice: x: 2, y: 2, z: 4, core: 2. Of those that a mesh axis runs over, the one named last changes fastest.
Arguments:
- env_left: bfloat16 [4, 56, 34, 128, 128], P('seg', 'sec'), may hold values from -6 to 6
- isometry: bfloat16 [1, 4, 56, 4, 128, 128], P(None, 'seg', 'sec'), may hold values from -0.25 to 0.25
- sing_vals: float32 [4, 56, 128], P('seg', 'sec'), may hold values from 0.5 to 2
- kept: int32 [1, 4, 56], P(None, 'seg', 'sec'), may hold values from 32 to 128
- twosite_sector: int32 [1, 4, 56], P(None, 'seg'), may hold values from 0 to 55, as said below
- mpo_row: int32 [34, 3], replicated, may hold values from 0 to 33
- mpo_op: int32 [34, 3], replicated, may hold values from 0 to 5
- op_table: float32 [6, 4, 4], replicated, may hold values from -6 to 6
Outputs:
- env_right: bfloat16 [4, 56, 34, 128, 128], P('seg', 'sec')
- handoff: bfloat16 [4, 56, 34, 128, 128], P('seg', 'sec')
Inputs may be any that keep to these rules, and one draw needn't show every extreme that they name: `twosite_sector`: each row along the last dimension is a permutation of the 56 sectors. The 7 positions n with the same n // 7 hold sectors q with 7 different values of q // 7.
All inputs are finite; a program needn't handle non-finite values.
Results may differ from a plain program's by a relative error of at most 0.0081.
Values may be sent and summed in bfloat16 or wider, within the bound.
A program may use at most 128 MiB of HBM per device.

v0:
```python
import functools

import jax
import jax.numpy as jnp
from jax import lax
from jax.experimental import pallas as pl
from jax.experimental.pallas import tpu as pltpu
from jax.sharding import PartitionSpec as P

SITES = 1
CHARGES = (0, 1, 1, 2)
VMEM_LIMIT = 56 * 1024 * 1024


def passed_along(block, axis, distance):
    devices = range(lax.axis_size(axis))
    route = [(i - distance, i) for i in devices if i - distance in devices]
    return lax.ppermute(block, axis, route)


def take_kernel(index_ref, src_ref, dst_ref):
    dst_ref[...] = src_ref[...]


def take_blocks(blocks, index):
    block = (1,) + blocks.shape[1:]
    zeros = (0,) * (blocks.ndim - 1)
    count = index.shape[0]
    return pl.pallas_call(
        take_kernel,
        grid_spec=pltpu.PrefetchScalarGridSpec(
            num_scalar_prefetch=1,
            grid=(count,),
            in_specs=[pl.BlockSpec(block, lambda i, index: (index[i],) + zeros)],
            out_specs=pl.BlockSpec(block, lambda i, index: (i,) + zeros),
        ),
        out_shape=jax.ShapeDtypeStruct((count,) + blocks.shape[1:], blocks.dtype),
        name="take_blocks",
    )(index, blocks)


def sector_kernel(
    slot, holder, kept, row, op, table, e0, e1, e2, iso, s_col, s_row, *rest
):
    out, hand, placed_t, mixer, left, prod = rest[-6:]
    width = e0.shape[0]
    blk = e0.shape[-1]
    nops = table.shape[0] // 16
    keep = kept[slot]
    inside = lax.broadcasted_iota(jnp.int32, (blk, blk), 1) < keep
    placed = []
    for s in range(4):
        value = jnp.where(inside, iso[s].astype(jnp.float32), 0.0)
        placed.append(value)
        placed_t[s * blk : (s + 1) * blk, :] = value.T.astype(jnp.bfloat16)
    for x in range(nops):
        for p in range(4):
            total = None
            for s in range(4):
                if CHARGES[p] == CHARGES[s]:
                    term = table[x * 16 + p * 4 + s] * placed[s]
                    total = term if total is None else total + term
            mixer[p * blk : (p + 1) * blk, x * blk : (x + 1) * blk] = total.astype(jnp.bfloat16)

    def bra_step(w, carry):
        rows = pl.ds(pl.multiple_of(w * blk, blk), blk)
        first = jnp.dot(placed_t[0:blk], e0[w], preferred_element_type=jnp.float32)
        middle = jnp.dot(placed_t[blk : 3 * blk], e1[w], preferred_element_type=jnp.float32)
        last = jnp.dot(placed_t[3 * blk :], e2[w], preferred_element_type=jnp.float32)
        left[rows, 0:blk] = first.astype(jnp.bfloat16)
        left[rows, blk : 2 * blk] = middle[:blk].astype(jnp.bfloat16)
        left[rows, 2 * blk : 3 * blk] = middle[blk:].astype(jnp.bfloat16)
        left[rows, 3 * blk :] = last.astype(jnp.bfloat16)
        return carry

    lax.fori_loop(0, width, bra_step, 0, unroll=2)

    parts = 2
    tall = width // parts * blk

    def ket_step(i, carry):
        rows = pl.ds(pl.multiple_of(i * tall, blk), tall)
        for x in range(0, nops, 2):
            pair = jnp.dot(
                left[rows, :],
                mixer[:, x * blk : (x + 2) * blk],
                preferred_element_type=jnp.float32,
            )
            prod[x, rows, :] = pair[:, :blk]
            prod[x + 1, rows, :] = pair[:, blk:]
        return carry

    lax.fori_loop(0, parts, ket_step, 0)

    scale = jnp.where(
        lax.broadcasted_iota(jnp.int32, (1, blk), 1) < keep, 1.0 / s_row[...], 0.0
    )
    scale = scale.astype(jnp.bfloat16).astype(jnp.float32)
    side = jnp.where(
        lax.broadcasted_iota(jnp.int32, (blk, 1), 0) < keep, 1.0 / s_col[...], 0.0
    )
    side = jnp.broadcast_to(side.astype(jnp.bfloat16).astype(jnp.float32), (blk, blk))
    scale = jnp.broadcast_to(scale, (blk, blk))

    def column_step(v, carry):
        total = None
        for t in range(3):
            start = pl.multiple_of(row[v * 3 + t] * blk, blk)
            term = prod[op[v * 3 + t], pl.ds(start, blk), :]
            total = term if total is None else total + term
        value = total.astype(jnp.bfloat16)
        out[v] = value
        hand[v] = (side * value.astype(jnp.float32) * scale).astype(jnp.bfloat16)
        return carry

    lax.fori_loop(0, width, column_step, 0, unroll=2)


def sector_call(slot, lower, isom, s_col, s_row, scalars, buffer, shape):
    sectors, width, blk = shape[1], shape[2], shape[3]
    nops = scalars[4].shape[0] // 16
    held = lambda i, holder, *rest: (holder[slot], 0, 0, 0)
    any_spec = pl.BlockSpec(memory_space=pl.ANY)
    in_specs = [
        pl.BlockSpec(
            (None,) * (array.ndim - 3) + (width, blk, blk),
            functools.partial(
                lambda lead, i, *rest: lead + (0, 0, 0), (0,) * (array.ndim - 4) + (index,)
            ),
        )
        for array, index in lower
    ]
    in_specs += [
        pl.BlockSpec((None, 4, blk, blk), held),
        pl.BlockSpec((None, blk, 1), lambda i, *rest: (slot, 0, 0)),
        pl.BlockSpec((None, 1, blk), lambda i, *rest: (slot, 0, 0)),
    ]
    operands = [array for array, _ in lower] + [isom, s_col, s_row]
    aliases = {}
    if buffer is not None:
        in_specs.append(any_spec)
        aliases = {len(scalars) + len(operands): 0}
        operands.append(buffer)
    flops = 2 * blk * blk * blk * width * 4 * (1 + nops)
    return pl.pallas_call(
        functools.partial(sector_kernel, slot),
        grid_spec=pltpu.PrefetchScalarGridSpec(
            num_scalar_prefetch=len(scalars),
            grid=(1,),
            in_specs=in_specs,
            out_specs=[
                pl.BlockSpec((None, None, width, blk, blk), lambda i, *rest: (0, slot, 0, 0, 0)),
                pl.BlockSpec((width, blk, blk), lambda i, *rest: (0, 0, 0)),
            ],
            scratch_shapes=[
                pltpu.VMEM((4 * blk, blk), jnp.bfloat16),
                pltpu.VMEM((4 * blk, nops * blk), jnp.bfloat16),
                pltpu.VMEM((width * blk, 4 * blk), jnp.bfloat16),
                pltpu.VMEM((nops, width * blk, blk), jnp.float32),
            ],
        ),
        out_shape=[
            jax.ShapeDtypeStruct((1, sectors, width, blk, blk), jnp.bfloat16),
            jax.ShapeDtypeStruct((width, blk, blk), jnp.bfloat16),
        ],
        input_output_aliases=aliases,
        compiler_params=pltpu.CompilerParams(vmem_limit_bytes=VMEM_LIMIT),
        cost_estimate=pl.CostEstimate(
            flops=flops, bytes_accessed=5 * width * blk * blk * 2, transcendentals=0
        ),
        name=f"sector_{slot}",
    )(*scalars, *operands)


def store_kernel(src_ref, *rest):
    rest[-1][...] = src_ref[...]


def store_call(slot, piece, buffer, sectors):
    width, blk = piece.shape[0], piece.shape[-1]
    half = width // 2
    in_specs = [pl.BlockSpec((half, blk, blk), lambda i: (i, 0, 0))]
    operands = [piece]
    aliases = {}
    if buffer is not None:
        in_specs.append(pl.BlockSpec(memory_space=pl.ANY))
        operands.append(buffer)
        aliases = {1: 0}
    return pl.pallas_call(
        store_kernel,
        grid=(2,),
        in_specs=in_specs,
        out_specs=pl.BlockSpec((None, None, half, blk, blk), lambda i: (0, slot, i, 0, 0)),
        out_shape=jax.ShapeDtypeStruct((1, sectors, width, blk, blk), jnp.bfloat16),
        input_output_aliases=aliases,
        cost_estimate=pl.CostEstimate(
            flops=0, bytes_accessed=2 * width * blk * blk * 2, transcendentals=0
        ),
        name=f"store_{slot}",
    )(*operands)


def body(env_left, isometry, sing_vals, kept, twosite_sector, mpo_row, mpo_op, op_table):
    my_index = lax.axis_index("sec")
    devices = lax.axis_size("sec")
    per_dev = env_left.shape[1]
    lower = passed_along(env_left[0, per_dev - 2 :], "sec", 1)

    sector_row = twosite_sector[0, 0]
    positions = jnp.arange(sector_row.shape[0], dtype=jnp.int32)
    owner = lax.dynamic_slice_in_dim(sector_row, my_index * per_dev, per_dev) // per_dev
    send = jnp.sum(
        jnp.where(
            owner[None, :] == jnp.arange(devices, dtype=jnp.int32)[:, None],
            jnp.arange(per_dev, dtype=jnp.int32)[None, :],
            0,
        ),
        axis=1,
    )
    mine = my_index * per_dev + jnp.arange(per_dev, dtype=jnp.int32)
    where_held = jnp.sum(
        jnp.where(sector_row[None, :] == mine[:, None], positions[None, :], 0), axis=1
    )
    holder = where_held // per_dev
    isom = lax.all_to_all(take_blocks(isometry[0, 0], send), "sec", 0, 0, tiled=True)

    scalars = (
        holder,
        kept[SITES - 1, 0],
        mpo_row.reshape(-1),
        mpo_op.reshape(-1),
        op_table.reshape(-1),
    )
    s_col = sing_vals[0][:, :, None]
    s_row = sing_vals[0][:, None, :]
    order = list(range(2, per_dev)) + [1, 0]
    env_right = None
    pieces = []
    for slot in order:
        below = [
            (env_left, slot - c) if slot >= c else (lower, slot - c + 2) for c in range(3)
        ]
        env_right, hand = sector_call(
            slot, below, isom, s_col, s_row, scalars, env_right, env_left.shape[:-1]
        )
        pieces.append(passed_along(hand, "seg", 1))
    handoff = None
    for slot, piece in zip(order, pieces):
        handoff = store_call(slot, piece, handoff, per_dev)
    return env_right, handoff


def solution(mesh):
    in_specs = (
        P("seg", "sec", None, None, None),
        P(None, "seg", "sec", None, None, None),
        P("seg", "sec", None),
        P(None, "seg", "sec"),
        P(None, "seg", None),
        P(),
        P(),
        P(),
    )
    out_specs = (P("seg", "sec", None, None, None), P("seg", "sec", None, None, None))
    return jax.shard_map(body, mesh=mesh, in_specs=in_specs, out_specs=out_specs, check_vma=False)
```

profile of v0, /device:TPU:10, one launch (start us, length us, event | category | flops | bytes accessed | tf_op | source)
XLA Modules:
  0.0 227.2 jit_solution(14041640728370163909)
XLA Ops:
  0.6 0.7 bitcast_select_fusion
  1.4 0.6 select_reduce_fusion.index_ref
  2.0 5.9 %take_blocks.1 = bf16[8,4,128,128]{3,2,1,0:T(8,128)(2,1)} custom-call(s32[8]{0:T(128)} %select_reduce_fusion.index_ref, bf16[7,4,128,128]{3,2,1,0:T(8,128)(2,1)} %bitcast.11), custom_call_target="tpu_custom_call" | custom-call | tf_op jit(solution)/shard_map/take_blocks/pallas_call | solution.py:29
  7.9 4.2 %all-to-all-start = ((bf16[8,4,128,128]{3,2,1,0:T(8,128)(2,1)}), bf16[8,4,128,128]{3,2,1,0:T(8,128)(2,1)S(1)}, u32[]{:S(2)}, u32[]{:S(2)}) async-start(bf16[8,4,128,128]{3,2,1,0:T(8,128)(2,1)} %take_blocks.1), calls=%async_computation | async-start | bytes 2097152 | tf_op jit(solution)/shard_map/all_to_all | solution.py:225
  12.1 0.0 copy-start.5
  12.1 0.0 copy-start.7
  12.1 0.0 copy-start.8
  12.1 0.0 copy-start.6
  12.1 0.0 copy-start.10
  12.1 3.3 %slice_bitcast_fusion = bf16[2,34,128,128]{3,2,1,0:T(8,128)(2,1)} fusion(bf16[1,7,34,128,128]{4,3,2,1,0:T(8,128)(2,1)} %e0.13), kind=kLoop, calls=%fused_computation | loop fusion | bytes 4456448 | tf_op jit(solution)/shard_map/squeeze | solution.py:207
  15.4 2.0 collective-permute-start
  17.5 0.0 copy-done.5
  17.5 1.0 copy.44.s_col
  18.5 0.0 copy-done.7
  18.5 0.1 copy.35
  18.6 0.6 reshape.47.row
  19.3 0.0 copy-done.8
  19.3 0.1 copy.36
  19.4 0.7 reshape.48.op
  20.1 0.0 copy-done.6
  20.1 0.1 copy.37
  20.2 0.6 reshape.49.table
  20.8 0.0 copy-done.10
  20.8 0.2 select_reduce_fusion.1
  21.0 0.5 and_select_fusion.holder
  21.5 4.5 %all-to-all-done.iso = bf16[8,4,128,128]{3,2,1,0:T(8,128)(2,1)S(1)} async-done(((bf16[8,4,128,128]{3,2,1,0:T(8,128)(2,1)}), bf16[8,4,128,128]{3,2,1,0:T(8,128)(2,1)S(1)}, u32[]{:S(2)}, u32[]{:S(2)}) %all-to-all-start) | async-done | bytes 1048608 | tf_op jit(solution)/shard_map/all_to_all | solution.py:225
  26.0 0.0 copy-start
  26.0 1.0 copy-done
  27.0 12.5 %sector_2.1 = (bf16[1,7,34,128,128]{4,3,2,1,0:T(8,128)(2,1)}, bf16[34,128,128]{2,1,0:T(8,128)(2,1)}) custom-call(s32[7]{0:T(128)} %and_select_fusion.holder, s32[7]{0:T(128)} %bitcast.20, s32[102]{0:T(128)} %reshape.47.row, s32[102]{0:T(128)} %reshape.48.op, f32[96]{0:T(128)} %reshape.49.table, bf16[1,7,34,128,128]{4,3,2,1,0:T(8,128)(2,1)} %e0.13, ...), custom_call_target="tpu_custom_call" | custom-call | flops 3992977408 | bytes 5570560 | tf_op jit(solution)/shard_map/sector_2/pallas_call | solution.py:145
  39.5 0.0 copy-start.9
  39.5 12.6 %sector_3.1 = (bf16[1,7,34,128,128]{4,3,2,1,0:T(8,128)(2,1)}, bf16[34,128,128]{2,1,0:T(8,128)(2,1)}) custom-call(s32[7]{0:T(128)} %and_select_fusion.holder, s32[7]{0:T(128)} %bitcast.21, s32[102]{0:T(128)} %reshape.47.row, s32[102]{0:T(128)} %reshape.48.op, f32[96]{0:T(128)} %reshape.49.table, ...), custom_call_target="tpu_custom_call", output_to_operand_aliasing={{0}: (11, {})} | custom-call | flops 3992977408 | bytes 5570560 | tf_op jit(solution)/shard_map/sector_3/pallas_call | solution.py:145
  52.2 3.5 %collective-permute-start.6 = (bf16[34,128,128]{2,1,0:T(8,128)(2,1)}, bf16[34,128,128]{2,1,0:T(8,128)(2,1)S(1)}, u32[]{:S(2)}, u32[]{:S(2)}) collective-permute-start(bf16[34,128,128]{2,1,0:T(8,128)(2,1)} %get-tuple-element.28), channel_id=1, source_target_pairs={{0,8},{8,16},{16,24},{1,9},{9,17},{17,25},{2,10},{10,18},{18,26},{... | collective-permute-start | bytes 3342344 | tf_op jit(solution)/shard_map/ppermute | solution.py:18
  55.7 0.0 copy-done.9
  55.7 3.5 %collective-permute-start.7 = (bf16[34,128,128]{2,1,0:T(8,128)(2,1)S(1)}, bf16[34,128,128]{2,1,0:T(8,128)(2,1)}, u32[]{:S(2)}, u32[]{:S(2)}) collective-permute-start(bf16[34,128,128]{2,1,0:T(8,128)(2,1)S(1)} %copy-done.9), channel_id=1, source_target_pairs={{0,8},{8,16},{16,24},{1,9},{9,17},{17,25},{2,10},{10,18},{18,26},{... | collective-permute-start | bytes 3342344 | tf_op jit(solution)/shard_map/ppermute | solution.py:18
  59.2 12.5 %sector_4.1 = (bf16[1,7,34,128,128]{4,3,2,1,0:T(8,128)(2,1)}, bf16[34,128,128]{2,1,0:T(8,128)(2,1)}) custom-call(s32[7]{0:T(128)} %and_select_fusion.holder, s32[7]{0:T(128)} %bitcast.22, s32[102]{0:T(128)} %reshape.47.row, s32[102]{0:T(128)} %reshape.48.op, f32[96]{0:T(128)} %reshape.49.table, ...), custom_call_target="tpu_custom_call", output_to_operand_aliasing={{0}: (11, {})} | custom-call | flops 3992977408 | bytes 5570560 | tf_op jit(solution)/shard_map/sector_4/pallas_call | solution.py:145
  71.7 1.9 collective-permute-start.5
  73.6 12.5 %sector_5.1 = (bf16[1,7,34,128,128]{4,3,2,1,0:T(8,128)(2,1)}, bf16[34,128,128]{2,1,0:T(8,128)(2,1)}) custom-call(s32[7]{0:T(128)} %and_select_fusion.holder, s32[7]{0:T(128)} %bitcast.23, s32[102]{0:T(128)} %reshape.47.row, s32[102]{0:T(128)} %reshape.48.op, f32[96]{0:T(128)} %reshape.49.table, ...), custom_call_target="tpu_custom_call", output_to_operand_aliasing={{0}: (11, {})} | custom-call | flops 3992977408 | bytes 5570560 | tf_op jit(solution)/shard_map/sector_5/pallas_call | solution.py:145
  86.2 2.1 collective-permute-start.4
  88.3 12.5 %sector_6.1 = (bf16[1,7,34,128,128]{4,3,2,1,0:T(8,128)(2,1)}, bf16[34,128,128]{2,1,0:T(8,128)(2,1)}) custom-call(s32[7]{0:T(128)} %and_select_fusion.holder, s32[7]{0:T(128)} %bitcast.24, s32[102]{0:T(128)} %reshape.47.row, s32[102]{0:T(128)} %reshape.48.op, f32[96]{0:T(128)} %reshape.49.table, ...), custom_call_target="tpu_custom_call", output_to_operand_aliasing={{0}: (11, {})} | custom-call | flops 3992977408 | bytes 5570560 | tf_op jit(solution)/shard_map/sector_6/pallas_call | solution.py:145
  100.8 0.0 collective-permute-done.e2.e1
  100.8 0.0 copy-start.1
  100.8 1.9 collective-permute-start.3
  102.7 0.0 copy-done.1
  102.7 12.6 %sector_1.1 = (bf16[1,7,34,128,128]{4,3,2,1,0:T(8,128)(2,1)}, bf16[34,128,128]{2,1,0:T(8,128)(2,1)}) custom-call(s32[7]{0:T(128)} %and_select_fusion.holder, s32[7]{0:T(128)} %bitcast.25, s32[102]{0:T(128)} %reshape.47.row, s32[102]{0:T(128)} %reshape.48.op, f32[96]{0:T(128)} %reshape.49.table, ...), custom_call_target="tpu_custom_call", output_to_operand_aliasing={{0}: (11, {})} | custom-call | flops 3992977408 | bytes 5570560 | tf_op jit(solution)/shard_map/sector_1/pallas_call | solution.py:145
  115.3 12.5 %sector_0.1 = (bf16[1,7,34,128,128]{4,3,2,1,0:T(8,128)(2,1)}, bf16[34,128,128]{2,1,0:T(8,128)(2,1)}) custom-call(s32[7]{0:T(128)} %and_select_fusion.holder, s32[7]{0:T(128)} %bitcast.26, s32[102]{0:T(128)} %reshape.47.row, s32[102]{0:T(128)} %reshape.48.op, f32[96]{0:T(128)} %reshape.49.table, ...), custom_call_target="tpu_custom_call", output_to_operand_aliasing={{0}: (11, {})} | custom-call | flops 3992977408 | bytes 5570560 | tf_op jit(solution)/shard_map/sector_0/pallas_call | solution.py:145
  127.8 0.0 collective-permute-done.6.src_ref
  127.8 1.9 collective-permute-start.2
  129.7 0.0 collective-permute-done.7.src_ref
  129.8 1.9 collective-permute-start.1
  131.7 2.1 store_2.1.rest_0_
  133.8 0.0 copy-done.2
  133.8 2.1 store_3.1.rest_0_
  135.8 0.0 collective-permute-done.5.src_ref
  135.9 2.1 store_4.1.rest_0_
  137.9 15.5 %collective-permute-done.4.src_ref = bf16[34,128,128]{2,1,0:T(8,128)(2,1)} collective-permute-done((bf16[34,128,128]{2,1,0:T(8,128)(2,1)}, bf16[34,128,128]{2,1,0:T(8,128)(2,1)}, u32[]{:S(2)}, u32[]{:S(2)}) %collective-permute-start.4) | collective-permute-done | bytes 1114144 | tf_op jit(solution)/shard_map/ppermute | solution.py:18
  153.4 2.1 store_5.1.rest_0_
  155.5 21.8 %collective-permute-done.3.src_ref = bf16[34,128,128]{2,1,0:T(8,128)(2,1)} collective-permute-done((bf16[34,128,128]{2,1,0:T(8,128)(2,1)}, bf16[34,128,128]{2,1,0:T(8,128)(2,1)}, u32[]{:S(2)}, u32[]{:S(2)}) %collective-permute-start.3) | collective-permute-done | bytes 1114144 | tf_op jit(solution)/shard_map/ppermute | solution.py:18
  177.3 2.1 store_6.1.rest_0_
  179.4 21.7 %collective-permute-done.2.src_ref = bf16[34,128,128]{2,1,0:T(8,128)(2,1)S(1)} collective-permute-done((bf16[34,128,128]{2,1,0:T(8,128)(2,1)}, bf16[34,128,128]{2,1,0:T(8,128)(2,1)S(1)}, u32[]{:S(2)}, u32[]{:S(2)}) %collective-permute-start.2) | collective-permute-done | bytes 1114144 | tf_op jit(solution)/shard_map/ppermute | solution.py:18
  201.1 1.0 copy-done.3
  202.1 2.1 store_1.1.rest_0_
  204.1 19.9 %collective-permute-done.1.src_ref = bf16[34,128,128]{2,1,0:T(8,128)(2,1)S(1)} collective-permute-done((bf16[34,128,128]{2,1,0:T(8,128)(2,1)}, bf16[34,128,128]{2,1,0:T(8,128)(2,1)S(1)}, u32[]{:S(2)}, u32[]{:S(2)}) %collective-permute-start.1) | collective-permute-done | bytes 1114144 | tf_op jit(solution)/shard_map/ppermute | solution.py:18
  224.1 1.0 copy-done.4
  225.1 2.1 store_0.1
  (4 shorter events, 0.0 us)
Async XLA Ops:
  7.9 18.1 %all-to-all-start = ((bf16[8,4,128,128]{3,2,1,0:T(8,128)(2,1)}), bf16[8,4,128,128]{3,2,1,0:T(8,128)(2,1)S(1)}, u32[]{:S(2)}, u32[]{:S(2)}) async-start(bf16[8,4,128,128]{3,2,1,0:T(8,128)(2,1)} %take_blocks.1), calls=%async_computation | async-start | bytes 2097152 | tf_op jit(solution)/shard_map/all_to_all | solution.py:225
  12.1 5.4 %copy-start.5 = (f32[1,7,128]{2,0,1:T(1,128)S(1)}, f32[1,7,128]{2,0,1:T(1,128)}, u32[]{:S(2)}) copy-start(f32[1,7,128]{2,0,1:T(1,128)} %param.10) | copy-start | bytes 10756
  12.1 6.4 %copy-start.7 = (s32[34,3]{0,1:T(4,128)S(1)}, s32[34,3]{0,1:T(4,128)}, u32[]{:S(2)}) copy-start(s32[34,3]{0,1:T(4,128)} %param.13) | copy-start | bytes 1228
  12.1 7.1 %copy-start.8 = (s32[34,3]{0,1:T(4,128)S(1)}, s32[34,3]{0,1:T(4,128)}, u32[]{:S(2)}) copy-start(s32[34,3]{0,1:T(4,128)} %param.14) | copy-start | bytes 1228
  12.1 7.9 %copy-start.6 = (f32[6,4,4]{0,2,1:T(4,128)S(1)}, f32[6,4,4]{0,2,1:T(4,128)}, u32[]{:S(2)}) copy-start(f32[6,4,4]{0,2,1:T(4,128)} %param.15) | copy-start | bytes 1156
  12.1 8.6 %copy-start.10 = (s32[1,1,56]{2,1,0:T(1,128)S(1)}, s32[1,1,56]{2,1,0:T(1,128)}, u32[]{:S(2)}) copy-start(s32[1,1,56]{2,1,0:T(1,128)} %param.12) | copy-start | bytes 676
  15.4 85.3 %collective-permute-start = (bf16[2,34,128,128]{3,2,1,0:T(8,128)(2,1)}, bf16[2,34,128,128]{3,2,1,0:T(8,128)(2,1)S(1)}, u32[]{:S(2)}, u32[]{:S(2)}) collective-permute-start(bf16[2,34,128,128]{3,2,1,0:T(8,128)(2,1)} %slice_bitcast_fusion), channel_id=1, source_target_pairs={{0,1},{1,2},{2,3},{3,4},{4,5},{5,6},{6,7},{8,9},{9,10},{10,11},{11... | collective-permute-start | bytes 6684680 | tf_op jit(solution)/shard_map/ppermute | solution.py:18
  26.0 1.0 copy-start
  39.5 16.1 %copy-start.9 = (bf16[34,128,128]{2,1,0:T(8,128)(2,1)S(1)}, bf16[34,128,128]{2,1,0:T(8,128)(2,1)}, u32[]{:S(2)}) copy-start(bf16[34,128,128]{2,1,0:T(8,128)(2,1)} %get-tuple-element.29) | copy-start | bytes 3342340
  52.2 75.6 %collective-permute-start.6 = (bf16[34,128,128]{2,1,0:T(8,128)(2,1)}, bf16[34,128,128]{2,1,0:T(8,128)(2,1)S(1)}, u32[]{:S(2)}, u32[]{:S(2)}) collective-permute-start(bf16[34,128,128]{2,1,0:T(8,128)(2,1)} %get-tuple-element.28), channel_id=1, source_target_pairs={{0,8},{8,16},{16,24},{1,9},{9,17},{17,25},{2,10},{10,18},{18,26},{... | collective-permute-start | bytes 3342344 | tf_op jit(solution)/shard_map/ppermute | solution.py:18
  55.7 74.1 %collective-permute-start.7 = (bf16[34,128,128]{2,1,0:T(8,128)(2,1)S(1)}, bf16[34,128,128]{2,1,0:T(8,128)(2,1)}, u32[]{:S(2)}, u32[]{:S(2)}) collective-permute-start(bf16[34,128,128]{2,1,0:T(8,128)(2,1)S(1)} %copy-done.9), channel_id=1, source_target_pairs={{0,8},{8,16},{16,24},{1,9},{9,17},{17,25},{2,10},{10,18},{18,26},{... | collective-permute-start | bytes 3342344 | tf_op jit(solution)/shard_map/ppermute | solution.py:18
  71.7 64.2 %collective-permute-start.5 = (bf16[34,128,128]{2,1,0:T(8,128)(2,1)}, bf16[34,128,128]{2,1,0:T(8,128)(2,1)}, u32[]{:S(2)}, u32[]{:S(2)}) collective-permute-start(bf16[34,128,128]{2,1,0:T(8,128)(2,1)} %get-tuple-element.27), channel_id=1, source_target_pairs={{0,8},{8,16},{16,24},{1,9},{9,17},{17,25},{2,10},{10,18},{18,26},{... | collective-permute-start | bytes 3342344 | tf_op jit(solution)/shard_map/ppermute | solution.py:18
  86.2 67.3 %collective-permute-start.4 = (bf16[34,128,128]{2,1,0:T(8,128)(2,1)}, bf16[34,128,128]{2,1,0:T(8,128)(2,1)}, u32[]{:S(2)}, u32[]{:S(2)}) collective-permute-start(bf16[34,128,128]{2,1,0:T(8,128)(2,1)} %get-tuple-element.26), channel_id=1, source_target_pairs={{0,8},{8,16},{16,24},{1,9},{9,17},{17,25},{2,10},{10,18},{18,26},{... | collective-permute-start | bytes 3342344 | tf_op jit(solution)/shard_map/ppermute | solution.py:18
  100.8 1.9 copy-start.1
  100.8 76.5 %collective-permute-start.3 = (bf16[34,128,128]{2,1,0:T(8,128)(2,1)}, bf16[34,128,128]{2,1,0:T(8,128)(2,1)}, u32[]{:S(2)}, u32[]{:S(2)}) collective-permute-start(bf16[34,128,128]{2,1,0:T(8,128)(2,1)} %get-tuple-element.25), channel_id=1, source_target_pairs={{0,8},{8,16},{16,24},{1,9},{9,17},{17,25},{2,10},{10,18},{18,26},{... | collective-permute-start | bytes 3342344 | tf_op jit(solution)/shard_map/ppermute | solution.py:18
  127.8 6.0 %copy-start.2 = (bf16[34,128,128]{2,1,0:T(8,128)(2,1)}, bf16[34,128,128]{2,1,0:T(8,128)(2,1)S(1)}, u32[]{:S(2)}) copy-start(bf16[34,128,128]{2,1,0:T(8,128)(2,1)S(1)} %collective-permute-done.6.src_ref) | copy-start | bytes 3342340
  127.8 73.2 %collective-permute-start.2 = (bf16[34,128,128]{2,1,0:T(8,128)(2,1)}, bf16[34,128,128]{2,1,0:T(8,128)(2,1)S(1)}, u32[]{:S(2)}, u32[]{:S(2)}) collective-permute-start(bf16[34,128,128]{2,1,0:T(8,128)(2,1)} %get-tuple-element.24), channel_id=1, source_target_pairs={{0,8},{8,16},{16,24},{1,9},{9,17},{17,25},{2,10},{10,18},{18,26},{... | collective-permute-start | bytes 3342344 | tf_op jit(solution)/shard_map/ppermute | solution.py:18
  129.8 94.3 %collective-permute-start.1 = (bf16[34,128,128]{2,1,0:T(8,128)(2,1)}, bf16[34,128,128]{2,1,0:T(8,128)(2,1)S(1)}, u32[]{:S(2)}, u32[]{:S(2)}) collective-permute-start(bf16[34,128,128]{2,1,0:T(8,128)(2,1)} %get-tuple-element.23), channel_id=1, source_target_pairs={{0,8},{8,16},{16,24},{1,9},{9,17},{17,25},{2,10},{10,18},{18,26},{... | collective-permute-start | bytes 3342344 | tf_op jit(solution)/shard_map/ppermute | solution.py:18
  201.1 1.0 copy-start.3
  224.1 1.0 copy-start.4
where the time goes:
time: 228 us; the launch traced here: 227 us
  Pallas kernels  108 us (47%)
  waiting for transfers between devices  83.4 us (37%)
  starting transfers between devices  23 us (10%)
  local copies, waits for them, and re-layouts  9.58 us (4%)
    pallas_call x7, Pallas kernels, sector_call(): pl.pallas_call(functools.partial(sector_kernel, slot), grid_spec=pltpu.Pr...  87.8 us
    ppermute x8, waiting for transfers between devices, passed_along(): return lax.ppermute(block, axis, route)  78.9 us
    ppermute x8, starting transfers between devices, passed_along(): return lax.ppermute(block, axis, route)  18.8 us
    pallas_call x7, Pallas kernels, store_call(): pl.pallas_call(store_kernel, grid=(2,), in_specs=in_specs, out_specs=pl.B...  14.6 us
    pallas_call x1, Pallas kernels, take_blocks(): pl.pallas_call(take_kernel, grid_spec=pltpu.PrefetchScalarGridSpec(num_sc...  5.88 us
  transfers between devices with their start and end apart: 9, of which 5 were waited for; matrix products, arithmetic and copies ran while one was open for 3% of the time, Pallas kernels for 44%

commit v1 on v0

v1 whole, which is shorter than its diff:
```python
import functools

import jax
import jax.numpy as jnp
from jax import lax
from jax.experimental import pallas as pl
from jax.experimental.pallas import tpu as pltpu
from jax.sharding import PartitionSpec as P

SITES = 1
CHARGES = (0, 1, 1, 2)
VMEM_LIMIT = 56 * 1024 * 1024


def passed_along(block, axis, distance):
    devices = range(lax.axis_size(axis))
    route = [(i - distance, i) for i in devices if i - distance in devices]
    return lax.ppermute(block, axis, route)


def take_kernel(index_ref, src_ref, dst_ref):
    for i in range(dst_ref.shape[0]):
        dst_ref[i] = src_ref[index_ref[i]]


def take_blocks(blocks, index):
    count = index.shape[0]
    return pl.pallas_call(
        take_kernel,
        in_specs=[
            pl.BlockSpec(memory_space=pltpu.SMEM),
            pl.BlockSpec(memory_space=pltpu.VMEM),
        ],
        out_specs=pl.BlockSpec(memory_space=pltpu.VMEM),
        out_shape=jax.ShapeDtypeStruct((count,) + blocks.shape[1:], blocks.dtype),
        name="take_blocks",
    )(index, blocks)


def store_copy(stored, src_ref, dst_ref, sem):
    slot, part = stored
    tile = src_ref.shape[1]
    rows = pl.ds(part * tile, tile)
    return pltpu.make_async_copy(src_ref, dst_ref.at[0, slot, :, rows, :], sem)


def sector_kernel(
    slot, first_row, stored, holder, kept, row, op, table, e0, e1, e2, iso, s_col, s_row, *rest
):
    placed_t, mixer, left, prod = rest[-5:-1]
    out, hand = rest[-8:-6] if stored else rest[-7:-5]
    copy = None
    if stored:
        copy = store_copy(stored, rest[0], rest[-6], rest[-1])
        copy.start()
    width = e0.shape[0]
    blk = e0.shape[-1]
    tile = out.shape[1]
    nops = table.shape[0] // 16
    keep = kept[slot]
    inside = lax.broadcasted_iota(jnp.int32, (blk, blk), 1) < keep
    placed = []
    for s in range(4):
        value = jnp.where(inside, iso[s].astype(jnp.float32), 0.0)
        placed.append(value)
        turned = value.T[first_row : first_row + tile]
        placed_t[s * tile : (s + 1) * tile, :] = turned.astype(jnp.bfloat16)
    for x in range(nops):
        for p in range(4):
            total = None
            for s in range(4):
                if CHARGES[p] == CHARGES[s]:
                    term = table[x * 16 + p * 4 + s] * placed[s]
                    total = term if total is None else total + term
            mixer[p * blk : (p + 1) * blk, x * blk : (x + 1) * blk] = total.astype(jnp.bfloat16)

    def bra_step(w, carry):
        rows = pl.ds(pl.multiple_of(w * tile, tile), tile)
        first = jnp.dot(placed_t[0:tile], e0[w], preferred_element_type=jnp.float32)
        middle = jnp.dot(placed_t[tile : 3 * tile], e1[w], preferred_element_type=jnp.float32)
        last = jnp.dot(placed_t[3 * tile :], e2[w], preferred_element_type=jnp.float32)
        left[rows, 0:blk] = first.astype(jnp.bfloat16)
        left[rows, blk : 2 * blk] = middle[:tile].astype(jnp.bfloat16)
        left[rows, 2 * blk : 3 * blk] = middle[tile:].astype(jnp.bfloat16)
        left[rows, 3 * blk :] = last.astype(jnp.bfloat16)
        return carry

    lax.fori_loop(0, width, bra_step, 0, unroll=2)

    parts = 2
    tall = width // parts * tile

    def ket_step(i, carry):
        rows = pl.ds(pl.multiple_of(i * tall, tile), tall)
        for x in range(0, nops, 2):
            pair = jnp.dot(
                left[rows, :],
                mixer[:, x * blk : (x + 2) * blk],
                preferred_element_type=jnp.float32,
            )
            prod[x, rows, :] = pair[:, :blk]
            prod[x + 1, rows, :] = pair[:, blk:]
        return carry

    lax.fori_loop(0, parts, ket_step, 0)

    scale = jnp.where(
        lax.broadcasted_iota(jnp.int32, (1, blk), 1) < keep, 1.0 / s_row[...], 0.0
    )
    scale = scale.astype(jnp.bfloat16).astype(jnp.float32)
    side = jnp.where(
        lax.broadcasted_iota(jnp.int32, (blk, 1), 0) < keep, 1.0 / s_col[...], 0.0
    )
    side = side.astype(jnp.bfloat16).astype(jnp.float32)[first_row : first_row + tile]
    side = jnp.broadcast_to(side, (tile, blk))
    scale = jnp.broadcast_to(scale, (tile, blk))

    def column_step(v, carry):
        total = None
        for t in range(3):
            start = pl.multiple_of(row[v * 3 + t] * tile, tile)
            term = prod[op[v * 3 + t], pl.ds(start, tile), :]
            total = term if total is None else total + term
        value = total.astype(jnp.bfloat16)
        out[v] = value
        hand[v] = (side * value.astype(jnp.float32) * scale).astype(jnp.bfloat16)
        return carry

    lax.fori_loop(0, width, column_step, 0, unroll=2)
    if copy is not None:
        copy.wait()


def sector_call(slot, part, parts, lower, isom, s_col, s_row, scalars, buffer, shape, arrived):
    sectors, width, blk = shape[1], shape[2], shape[3]
    nops = scalars[4].shape[0] // 16
    tile = blk // parts
    held = lambda i, holder, *rest: (holder[slot], 0, 0, 0)
    any_spec = pl.BlockSpec(memory_space=pl.ANY)
    in_specs = [
        pl.BlockSpec(
            (None,) * (array.ndim - 3) + (width, blk, blk),
            functools.partial(
                lambda lead, i, *rest: lead + (0, 0, 0), (0,) * (array.ndim - 4) + (index,)
            ),
        )
        for array, index in lower
    ]
    in_specs += [
        pl.BlockSpec((None, 4, blk, blk), held),
        pl.BlockSpec((None, blk, 1), lambda i, *rest: (slot, 0, 0)),
        pl.BlockSpec((None, 1, blk), lambda i, *rest: (slot, 0, 0)),
    ]
    operands = [array for array, _ in lower] + [isom, s_col, s_row]
    stored, piece, handoff = arrived
    extra = [piece] if stored else []
    aliases = {}
    for index, array in ((0, buffer), (2, handoff)):
        if array is not None:
            aliases[len(scalars) + len(operands) + len(extra)] = index
            extra.append(array)
    in_specs += [any_spec] * len(extra)
    operands += extra
    whole = jax.ShapeDtypeStruct((1, sectors, width, blk, blk), jnp.bfloat16)
    flops = 2 * tile * blk * blk * width
    return pl.pallas_call(
        functools.partial(sector_kernel, slot, part * tile, stored),
        grid_spec=pltpu.PrefetchScalarGridSpec(
            num_scalar_prefetch=len(scalars),
            grid=(1,),
            in_specs=in_specs,
            out_specs=[
                pl.BlockSpec(
                    (None, None, width, tile, blk), lambda i, *rest: (0, slot, 0, part, 0)
                ),
                pl.BlockSpec((width, tile, blk), lambda i, *rest: (0, 0, 0)),
            ]
            + [any_spec] * bool(stored),
            scratch_shapes=[
                pltpu.VMEM((4 * tile, blk), jnp.bfloat16),
                pltpu.VMEM((4 * blk, nops * blk), jnp.bfloat16),
                pltpu.VMEM((width * tile, 4 * blk), jnp.bfloat16),
                pltpu.VMEM((nops, width * tile, blk), jnp.float32),
                pltpu.SemaphoreType.DMA,
            ],
        ),
        out_shape=[whole, jax.ShapeDtypeStruct((width, tile, blk), jnp.bfloat16)]
        + [whole] * bool(stored),
        input_output_aliases=aliases,
        compiler_params=pltpu.CompilerParams(vmem_limit_bytes=VMEM_LIMIT),
        cost_estimate=pl.CostEstimate(
            flops=flops, bytes_accessed=width * tile * blk, transcendentals=0
        ),
        name=f"sector_{slot}_{part}",
    )(*scalars, *operands)


def store_kernel(stored, src_ref, *rest):
    dst_ref, sem = rest[-2:]
    copy = store_copy(stored, src_ref, dst_ref, sem)
    copy.start()
    copy.wait()


def store_call(slot, part, piece, buffer, sectors):
    width, tile, blk = piece.shape
    any_spec = pl.BlockSpec(memory_space=pl.ANY)
    operands = [piece] if buffer is None else [piece, buffer]
    return pl.pallas_call(
        functools.partial(store_kernel, (slot, part)),
        in_specs=[any_spec] * len(operands),
        out_specs=any_spec,
        out_shape=jax.ShapeDtypeStruct((1, sectors, width, blk, blk), jnp.bfloat16),
        scratch_shapes=[pltpu.SemaphoreType.DMA],
        input_output_aliases={} if buffer is None else {1: 0},
        cost_estimate=pl.CostEstimate(
            flops=0, bytes_accessed=2 * width * tile * blk * 2, transcendentals=0
        ),
        name=f"store_{slot}_{part}",
    )(*operands)


def body(env_left, isometry, sing_vals, kept, twosite_sector, mpo_row, mpo_op, op_table):
    my_index = lax.axis_index("sec")
    devices = lax.axis_size("sec")
    per_dev = env_left.shape[1]
    sector_row = twosite_sector[0, 0]
    positions = jnp.arange(sector_row.shape[0], dtype=jnp.int32)
    owner = lax.dynamic_slice_in_dim(sector_row, my_index * per_dev, per_dev) // per_dev
    send = jnp.sum(
        jnp.where(
            owner[None, :] == jnp.arange(devices, dtype=jnp.int32)[:, None],
            jnp.arange(per_dev, dtype=jnp.int32)[None, :],
            0,
        ),
        axis=1,
    )
    mine = my_index * per_dev + jnp.arange(per_dev, dtype=jnp.int32)
    where_held = jnp.sum(
        jnp.where(sector_row[None, :] == mine[:, None], positions[None, :], 0), axis=1
    )
    holder = where_held // per_dev
    isom = lax.all_to_all(take_blocks(isometry[0, 0], send), "sec", 0, 0, tiled=True)
    late_env, _ = lax.optimization_barrier((env_left[0, per_dev - 2 :], isom))
    lower = passed_along(late_env, "sec", 1)

    scalars = (
        holder,
        kept[SITES - 1, 0],
        mpo_row.reshape(-1),
        mpo_op.reshape(-1),
        op_table.reshape(-1),
    )
    s_col = sing_vals[0][:, :, None]
    s_row = sing_vals[0][:, None, :]
    order = [(2, 0, 2), (2, 1, 2)]
    order += [(slot, 0, 1) for slot in list(range(3, per_dev)) + [1, 0]]
    env_right = handoff = None
    waiting = []
    for step, (slot, part, parts) in enumerate(order):
        below = [
            (env_left, slot - c) if slot >= c else (lower, slot - c + 2) for c in range(3)
        ]
        arrived = (None, None, None)
        if step == 2 or step > 2 and len(waiting) > 1:
            arrived = waiting.pop(0) + (handoff,)
        results = sector_call(
            slot,
            part,
            parts,
            below,
            isom,
            s_col,
            s_row,
            scalars,
            env_right,
            env_left.shape[:-1],
            arrived,
        )
        env_right, hand = results[:2]
        handoff = results[2] if arrived[0] else handoff
        waiting.append(((slot, part), passed_along(hand, "seg", 1)))
    for (slot, part), piece in waiting:
        handoff = store_call(slot, part, piece, handoff, per_dev)
    return env_right, handoff


def solution(mesh):
    in_specs = (
        P("seg", "sec", None, None, None),
        P(None, "seg", "sec", None, None, None),
        P("seg", "sec", None),
        P(None, "seg", "sec"),
        P(None, "seg", None),
        P(),
        P(),
        P(),
    )
    out_specs = (P("seg", "sec", None, None, None), P("seg", "sec", None, None, None))
    return jax.shard_map(body, mesh=mesh, in_specs=in_specs, out_specs=out_specs, check_vma=False)
```

time: 228 us -> 349 us (1.53)
  Pallas kernels: 108 us -> 291 us
  waiting for transfers between devices: 83.4 us -> 6.52 us
  local copies, waits for them, and re-layouts: 9.58 us -> 17.3 us
    pallas_call x15 -> x11, Pallas kernels: 108 us -> 291 us  [the longest x8 219 us: sector_call(): pl.pallas_call(functools.partial(sector_kernel, slot, part * tile, stored...]
    ppermute x8 -> x9, waiting for transfers between devices: 78.9 us -> 0.02 us  [passed_along(): return lax.ppermute(block, axis, route)]
    unnamed x25 -> x23, local copies, waits for them, and re-layouts: 3.36 us -> 11.8 us
    ppermute x8 -> x9, starting transfers between devices: 18.8 us -> 21.9 us  [passed_along(): return lax.ppermute(block, axis, route)]
  transfers between devices with their start and end apart: 9 -> 10, of which waited for: 5 -> 1; matrix products, arithmetic and copies ran while one was open for 3% -> 3% of each run, Pallas kernels for 44% -> 71%
where the time goes in v1:
time: 349 us; the launch traced here: 345 us
  Pallas kernels  291 us (83%)
  starting transfers between devices  26.1 us (7%)
  local copies, waits for them, and re-layouts  17.3 us (5%)
  waiting for transfers between devices  6.52 us (2%)
    pallas_call x8, Pallas kernels, sector_call(): pl.pallas_call(functools.partial(sector_kernel, slot, part * tile, stored...  219 us
    pallas_call x2, Pallas kernels, store_call(): pl.pallas_call(functools.partial(store_kernel, (slot, part)), in_specs=[a...  69.7 us
    ppermute x9, starting transfers between devices, passed_along(): return lax.ppermute(block, axis, route)  21.9 us
    unnamed x23, local copies, waits for them, and re-layouts  11.8 us
  transfers between devices with their start and end apart: 10, of which 1 were waited for; matrix products, arithmetic and copies ran while one was open for 3% of the time, Pallas kernels for 71%

profile of v1, /device:TPU:10, one launch (start us, length us, event | category | flops | bytes accessed | tf_op | source)
XLA Modules:
  0.0 344.9 jit_solution(9949674796673553693)
XLA Ops:
  0.6 0.7 bitcast_select_fusion
  1.4 0.6 select_reduce_fusion.index_ref
  2.0 2.2 take_blocks.1
  4.2 4.3 %all-to-all-start = ((bf16[8,4,128,128]{3,2,1,0:T(8,128)(2,1)}), bf16[8,4,128,128]{3,2,1,0:T(8,128)(2,1)S(1)}, u32[]{:S(2)}, u32[]{:S(2)}) async-start(bf16[8,4,128,128]{3,2,1,0:T(8,128)(2,1)} %take_blocks.1), calls=%async_computation | async-start | bytes 2097152 | tf_op jit(solution)/shard_map/all_to_all | solution.py:243
  8.5 0.8 copy.40
  9.3 0.6 reshape.49.table
  9.9 0.8 copy.38
  10.7 0.6 reshape.47.row
  11.3 0.8 copy.39
  12.1 0.7 reshape.48.op
  12.8 1.7 copy.48.s_col
  14.5 0.8 select_reduce_fusion.1
  15.3 0.6 and_select_fusion.holder
  15.9 6.5 %all-to-all-done.iso = bf16[8,4,128,128]{3,2,1,0:T(8,128)(2,1)S(1)} async-done(((bf16[8,4,128,128]{3,2,1,0:T(8,128)(2,1)}), bf16[8,4,128,128]{3,2,1,0:T(8,128)(2,1)S(1)}, u32[]{:S(2)}, u32[]{:S(2)}) %all-to-all-start) | async-done | bytes 1048608 | tf_op jit(solution)/shard_map/all_to_all | solution.py:243
  22.4 0.0 copy-start
  22.4 1.0 copy-done
  23.4 9.7 %sector_2_0.1 = (bf16[1,7,34,128,128]{4,3,2,1,0:T(8,128)(2,1)}, bf16[34,64,128]{2,1,0:T(8,128)(2,1)}) custom-call(s32[7]{0:T(128)} %and_select_fusion.holder, s32[7]{0:T(128)} %bitcast.21, s32[102]{0:T(128)} %reshape.47.row, s32[102]{0:T(128)} %reshape.48.op, f32[96]{0:T(128)} %reshape.49.table, bf16[1,7,34,128,128]{4,3,2,1,0:T(8,128)(2,1)} %e0.15, ...), custom_call_target="tpu_custom_call" | custom-call | flops 71303168 | bytes 278528 | tf_op jit(solution)/shard_map/sector_2_0/pallas_call | solution.py:166
  33.1 3.5 %collective-permute-start.2 = (bf16[34,64,128]{2,1,0:T(8,128)(2,1)}, bf16[34,64,128]{2,1,0:T(8,128)(2,1)S(1)}, u32[]{:S(2)}, u32[]{:S(2)}) collective-permute-start(bf16[34,64,128]{2,1,0:T(8,128)(2,1)} %get-tuple-element.28), channel_id=1, source_target_pairs={{0,8},{8,16},{16,24},{1,9},{9,17},{17,25},{2,10},{10,18},{18,26},{... | collective-permute-start | bytes 1671176 | tf_op jit(solution)/shard_map/ppermute | solution.py:18
  36.6 9.8 %sector_2_1.1 = (bf16[1,7,34,128,128]{4,3,2,1,0:T(8,128)(2,1)}, bf16[34,64,128]{2,1,0:T(8,128)(2,1)}) custom-call(s32[7]{0:T(128)} %and_select_fusion.holder, s32[7]{0:T(128)} %bitcast.22, s32[102]{0:T(128)} %reshape.47.row, s32[102]{0:T(128)} %reshape.48.op, f32[96]{0:T(128)} %reshape.49.table, ...), custom_call_target="tpu_custom_call", output_to_operand_aliasing={{0}: (11, {})} | custom-call | flops 71303168 | bytes 278528 | tf_op jit(solution)/shard_map/sector_2_1/pallas_call | solution.py:166
  46.4 3.5 %collective-permute-start.1 = (bf16[34,64,128]{2,1,0:T(8,128)(2,1)}, bf16[34,64,128]{2,1,0:T(8,128)(2,1)S(1)}, u32[]{:S(2)}, u32[]{:S(2)}) collective-permute-start(bf16[34,64,128]{2,1,0:T(8,128)(2,1)} %get-tuple-element.27), channel_id=1, source_target_pairs={{0,8},{8,16},{16,24},{1,9},{9,17},{17,25},{2,10},{10,18},{18,26},{... | collective-permute-start | bytes 1671176 | tf_op jit(solution)/shard_map/ppermute | solution.py:18
  49.9 1.9 slice_bitcast_fusion
  51.8 0.0 collective-permute-done.2.rest_0_
  51.8 0.0 copy-start.9
  51.8 0.8 copy-done.9
  52.6 22.0 %sector_3_0.1 = (bf16[1,7,34,128,128]{4,3,2,1,0:T(8,128)(2,1)}, bf16[34,128,128]{2,1,0:T(8,128)(2,1)}, bf16[1,7,34,128,128]{4,3,2,1,0:T(8,128)(2,1)}) custom-call(s32[7]{0:T(128)} %and_select_fusion.holder, s32[7]{0:T(128)} %bitcast.23, s32[102]{0:T(128)} %reshape.47.row, s32[102]{0:T(128)} %reshape.48.op, ...), custom_call_target="tpu_custom_call", output_to_operand_aliasing={{0}: (12, {})} | custom-call | flops 142606336 | bytes 557056 | tf_op jit(solution)/shard_map/sector_3_0/pallas_call | solution.py:166
  74.7 1.9 collective-permute-start.4
  76.6 1.9 collective-permute-start
  78.5 0.0 collective-permute-done.1.rest_0_
  78.6 0.0 copy-start.8
  78.6 0.8 copy-done.8
  79.4 22.0 %sector_4_0.1 = (bf16[1,7,34,128,128]{4,3,2,1,0:T(8,128)(2,1)}, bf16[34,128,128]{2,1,0:T(8,128)(2,1)}, bf16[1,7,34,128,128]{4,3,2,1,0:T(8,128)(2,1)}) custom-call(s32[7]{0:T(128)} %and_select_fusion.holder, s32[7]{0:T(128)} %bitcast.24, s32[102]{0:T(128)} %reshape.47.row, s32[102]{0:T(128)} %reshape.48.op, ...), custom_call_target="tpu_custom_call", output_to_operand_aliasing={{0}: (12, {}), {2}: (13, {})} | custom-call | flops 142606336 | bytes 557056 | tf_op jit(solution)/shard_map/sector_4_0/pallas_call | solution.py:166
  101.4 3.2 collective-permute-start.3
  104.6 0.0 collective-permute-done.4.rest_0_
  104.6 0.0 copy-start.3
  104.6 1.0 copy-done.3
  105.6 38.9 %sector_5_0.1 = (bf16[1,7,34,128,128]{4,3,2,1,0:T(8,128)(2,1)}, bf16[34,128,128]{2,1,0:T(8,128)(2,1)}, bf16[1,7,34,128,128]{4,3,2,1,0:T(8,128)(2,1)}) custom-call(s32[7]{0:T(128)} %and_select_fusion.holder, s32[7]{0:T(128)} %bitcast.25, s32[102]{0:T(128)} %reshape.47.row, s32[102]{0:T(128)} %reshape.48.op, ...), custom_call_target="tpu_custom_call", output_to_operand_aliasing={{0}: (12, {}), {2}: (13, {})} | custom-call | flops 142606336 | bytes 557056 | tf_op jit(solution)/shard_map/sector_5_0/pallas_call | solution.py:166
  144.5 2.1 collective-permute-start.6
  146.6 0.0 collective-permute-done.3.rest_0_
  146.6 0.0 copy-start.6
  146.7 1.0 copy-done.6
  147.7 38.9 %sector_6_0.1 = (bf16[1,7,34,128,128]{4,3,2,1,0:T(8,128)(2,1)}, bf16[34,128,128]{2,1,0:T(8,128)(2,1)}, bf16[1,7,34,128,128]{4,3,2,1,0:T(8,128)(2,1)}) custom-call(s32[7]{0:T(128)} %and_select_fusion.holder, s32[7]{0:T(128)} %bitcast.26, s32[102]{0:T(128)} %reshape.47.row, s32[102]{0:T(128)} %reshape.48.op, ...), custom_call_target="tpu_custom_call", output_to_operand_aliasing={{0}: (12, {}), {2}: (13, {})} | custom-call | flops 142606336 | bytes 557056 | tf_op jit(solution)/shard_map/sector_6_0/pallas_call | solution.py:166
  186.6 1.9 collective-permute-start.5
  188.5 0.0 collective-permute-done.e2.e1
  188.5 0.0 copy-start.1
  188.5 0.0 collective-permute-done.6.rest_0_
  188.5 0.0 copy-start.4
  188.6 1.4 copy-done.1
  189.9 0.4 copy-done.4
  190.3 38.9 %sector_1_0.1 = (bf16[1,7,34,128,128]{4,3,2,1,0:T(8,128)(2,1)}, bf16[34,128,128]{2,1,0:T(8,128)(2,1)}, bf16[1,7,34,128,128]{4,3,2,1,0:T(8,128)(2,1)}) custom-call(s32[7]{0:T(128)} %and_select_fusion.holder, s32[7]{0:T(128)} %bitcast.27, s32[102]{0:T(128)} %reshape.47.row, s32[102]{0:T(128)} %reshape.48.op, ...), custom_call_target="tpu_custom_call", output_to_operand_aliasing={{0}: (12, {}), {2}: (13, {})} | custom-call | flops 142606336 | bytes 557056 | tf_op jit(solution)/shard_map/sector_1_0/pallas_call | solution.py:166
  229.2 1.9 collective-permute-start.8
  231.1 0.0 collective-permute-done.5.rest_0_
  231.1 0.0 copy-start.2
  231.1 1.0 copy-done.2
  232.1 38.9 %sector_0_0.1 = (bf16[1,7,34,128,128]{4,3,2,1,0:T(8,128)(2,1)}, bf16[34,128,128]{2,1,0:T(8,128)(2,1)}, bf16[1,7,34,128,128]{4,3,2,1,0:T(8,128)(2,1)}) custom-call(s32[7]{0:T(128)} %and_select_fusion.holder, s32[7]{0:T(128)} %bitcast.28, s32[102]{0:T(128)} %reshape.47.row, s32[102]{0:T(128)} %reshape.48.op, ...), custom_call_target="tpu_custom_call", output_to_operand_aliasing={{0}: (12, {}), {2}: (13, {})} | custom-call | flops 142606336 | bytes 557056 | tf_op jit(solution)/shard_map/sector_0_0/pallas_call | solution.py:166
  271.0 1.9 collective-permute-start.7
  273.0 0.0 collective-permute-done.8.src_ref
  273.0 0.0 copy-start.5
  273.0 1.0 copy-done.5
  274.0 34.9 %store_1_0.1.rest_0_ = bf16[1,7,34,128,128]{4,3,2,1,0:T(8,128)(2,1)} custom-call(bf16[34,128,128]{2,1,0:T(8,128)(2,1)} %copy-done.5, bf16[1,7,34,128,128]{4,3,2,1,0:T(8,128)(2,1)} %get-tuple-element.47.rest_0_), custom_call_target="tpu_custom_call", output_to_operand_aliasing={{}: (1, {})} | custom-call | bytes 2228224 | tf_op jit(solution)/shard_map/store_1_0/pallas_call | solution.py:209
  308.9 0.0 collective-permute-done.7.src_ref
  308.9 0.0 copy-start.7
  308.9 1.0 copy-done.7
  309.9 34.9 %store_0_0.1 = bf16[1,7,34,128,128]{4,3,2,1,0:T(8,128)(2,1)} custom-call(bf16[34,128,128]{2,1,0:T(8,128)(2,1)} %copy-done.7, bf16[1,7,34,128,128]{4,3,2,1,0:T(8,128)(2,1)} %store_1_0.1.rest_0_), custom_call_target="tpu_custom_call", output_to_operand_aliasing={{}: (1, {})} | custom-call | bytes 2228224 | tf_op jit(solution)/shard_map/store_0_0/pallas_call | solution.py:209
  (1 shorter events, 0.0 us)
Async XLA Ops:
  4.2 18.2 %all-to-all-start = ((bf16[8,4,128,128]{3,2,1,0:T(8,128)(2,1)}), bf16[8,4,128,128]{3,2,1,0:T(8,128)(2,1)S(1)}, u32[]{:S(2)}, u32[]{:S(2)}) async-start(bf16[8,4,128,128]{3,2,1,0:T(8,128)(2,1)} %take_blocks.1), calls=%async_computation | async-start | bytes 2097152 | tf_op jit(solution)/shard_map/all_to_all | solution.py:243
  22.4 1.0 copy-start
  33.1 18.7 %collective-permute-start.2 = (bf16[34,64,128]{2,1,0:T(8,128)(2,1)}, bf16[34,64,128]{2,1,0:T(8,128)(2,1)S(1)}, u32[]{:S(2)}, u32[]{:S(2)}) collective-permute-start(bf16[34,64,128]{2,1,0:T(8,128)(2,1)} %get-tuple-element.28), channel_id=1, source_target_pairs={{0,8},{8,16},{16,24},{1,9},{9,17},{17,25},{2,10},{10,18},{18,26},{... | collective-permute-start | bytes 1671176 | tf_op jit(solution)/shard_map/ppermute | solution.py:18
  46.4 32.1 %collective-permute-start.1 = (bf16[34,64,128]{2,1,0:T(8,128)(2,1)}, bf16[34,64,128]{2,1,0:T(8,128)(2,1)S(1)}, u32[]{:S(2)}, u32[]{:S(2)}) collective-permute-start(bf16[34,64,128]{2,1,0:T(8,128)(2,1)} %get-tuple-element.27), channel_id=1, source_target_pairs={{0,8},{8,16},{16,24},{1,9},{9,17},{17,25},{2,10},{10,18},{18,26},{... | collective-permute-start | bytes 1671176 | tf_op jit(solution)/shard_map/ppermute | solution.py:18
  51.8 0.8 copy-start.9
  74.7 29.9 %collective-permute-start.4 = (bf16[34,128,128]{2,1,0:T(8,128)(2,1)}, bf16[34,128,128]{2,1,0:T(8,128)(2,1)S(1)}, u32[]{:S(2)}, u32[]{:S(2)}) collective-permute-start(bf16[34,128,128]{2,1,0:T(8,128)(2,1)} %get-tuple-element.33), channel_id=1, source_target_pairs={{0,8},{8,16},{16,24},{1,9},{9,17},{17,25},{2,10},{10,18},{18,26},{... | collective-permute-start | bytes 3342344 | tf_op jit(solution)/shard_map/ppermute | solution.py:18
  76.6 111.9 %collective-permute-start = (bf16[2,34,128,128]{3,2,1,0:T(8,128)(2,1)S(1)}, bf16[2,34,128,128]{3,2,1,0:T(8,128)(2,1)S(1)}, u32[]{:S(2)}, u32[]{:S(2)}) collective-permute-start(bf16[2,34,128,128]{3,2,1,0:T(8,128)(2,1)S(1)} %slice_bitcast_fusion), channel_id=1, source_target_pairs={{0,1},{1,2},{2,3},{3,4},{4,5},{5,6},{6,7},{8,9},{9,10},{10,11},{11... | collective-permute-start | bytes 6684680 | tf_op jit(solution)/shard_map/ppermute | solution.py:18
  78.6 0.8 copy-start.8
  101.4 45.3 %collective-permute-start.3 = (bf16[34,128,128]{2,1,0:T(8,128)(2,1)}, bf16[34,128,128]{2,1,0:T(8,128)(2,1)S(1)}, u32[]{:S(2)}, u32[]{:S(2)}) collective-permute-start(bf16[34,128,128]{2,1,0:T(8,128)(2,1)} %get-tuple-element.32), channel_id=1, source_target_pairs={{0,8},{8,16},{16,24},{1,9},{9,17},{17,25},{2,10},{10,18},{18,26},{... | collective-permute-start | bytes 3342344 | tf_op jit(solution)/shard_map/ppermute | solution.py:18
  104.6 1.0 copy-start.3
  144.5 44.0 %collective-permute-start.6 = (bf16[34,128,128]{2,1,0:T(8,128)(2,1)}, bf16[34,128,128]{2,1,0:T(8,128)(2,1)S(1)}, u32[]{:S(2)}, u32[]{:S(2)}) collective-permute-start(bf16[34,128,128]{2,1,0:T(8,128)(2,1)} %get-tuple-element.39), channel_id=1, source_target_pairs={{0,8},{8,16},{16,24},{1,9},{9,17},{17,25},{2,10},{10,18},{18,26},{... | collective-permute-start | bytes 3342344 | tf_op jit(solution)/shard_map/ppermute | solution.py:18
  146.6 1.0 copy-start.6
  186.6 44.5 %collective-permute-start.5 = (bf16[34,128,128]{2,1,0:T(8,128)(2,1)}, bf16[34,128,128]{2,1,0:T(8,128)(2,1)S(1)}, u32[]{:S(2)}, u32[]{:S(2)}) collective-permute-start(bf16[34,128,128]{2,1,0:T(8,128)(2,1)} %get-tuple-element.38), channel_id=1, source_target_pairs={{0,8},{8,16},{16,24},{1,9},{9,17},{17,25},{2,10},{10,18},{18,26},{... | collective-permute-start | bytes 3342344 | tf_op jit(solution)/shard_map/ppermute | solution.py:18
  188.5 1.4 copy-start.1
  188.5 1.7 copy-start.4
  229.2 43.8 %collective-permute-start.8 = (bf16[34,128,128]{2,1,0:T(8,128)(2,1)}, bf16[34,128,128]{2,1,0:T(8,128)(2,1)S(1)}, u32[]{:S(2)}, u32[]{:S(2)}) collective-permute-start(bf16[34,128,128]{2,1,0:T(8,128)(2,1)} %get-tuple-element.46), channel_id=1, source_target_pairs={{0,8},{8,16},{16,24},{1,9},{9,17},{17,25},{2,10},{10,18},{18,26},{... | collective-permute-start | bytes 3342344 | tf_op jit(solution)/shard_map/ppermute | solution.py:18
  231.1 1.0 copy-start.2
  271.0 37.8 %collective-permute-start.7 = (bf16[34,128,128]{2,1,0:T(8,128)(2,1)}, bf16[34,128,128]{2,1,0:T(8,128)(2,1)S(1)}, u32[]{:S(2)}, u32[]{:S(2)}) collective-permute-start(bf16[34,128,128]{2,1,0:T(8,128)(2,1)} %get-tuple-element.45), channel_id=1, source_target_pairs={{0,8},{8,16},{16,24},{1,9},{9,17},{17,25},{2,10},{10,18},{18,26},{... | collective-permute-start | bytes 3342344 | tf_op jit(solution)/shard_map/ppermute | solution.py:18
  273.0 1.0 copy-start.5
  308.9 1.0 copy-start.7

commit v2 on v1

--- a/solution.py
+++ b/solution.py
@@ -85,7 +85,7 @@
         left[rows, 3 * blk :] = last.astype(jnp.bfloat16)
         return carry
 
-    lax.fori_loop(0, width, bra_step, 0, unroll=2)
+    lax.fori_loop(0, width, bra_step, 0, unroll=width // 2)
 
     parts = 2
     tall = width // parts * tile
@@ -159,7 +159,9 @@
         if array is not None:
             aliases[len(scalars) + len(operands) + len(extra)] = index
             extra.append(array)
-    in_specs += [any_spec] * len(extra)
+    if stored:
+        in_specs.append(pl.BlockSpec(piece.shape, lambda i, *rest: (0, 0, 0)))
+    in_specs += [any_spec] * (len(extra) - bool(stored))
     operands += extra
     whole = jax.ShapeDtypeStruct((1, sectors, width, blk, blk), jnp.bfloat16)
     flops = 2 * tile * blk * blk * width
@@ -195,31 +197,6 @@
     )(*scalars, *operands)
 
 
-def store_kernel(stored, src_ref, *rest):
-    dst_ref, sem = rest[-2:]
-    copy = store_copy(stored, src_ref, dst_ref, sem)
-    copy.start()
-    copy.wait()
-
-
-def store_call(slot, part, piece, buffer, sectors):
-    width, tile, blk = piece.shape
-    any_spec = pl.BlockSpec(memory_space=pl.ANY)
-    operands = [piece] if buffer is None else [piece, buffer]
-    return pl.pallas_call(
-        functools.partial(store_kernel, (slot, part)),
-        in_specs=[any_spec] * len(operands),
-        out_specs=any_spec,
-        out_shape=jax.ShapeDtypeStruct((1, sectors, width, blk, blk), jnp.bfloat16),
-        scratch_shapes=[pltpu.SemaphoreType.DMA],
-        input_output_aliases={} if buffer is None else {1: 0},
-        cost_estimate=pl.CostEstimate(
-            flops=0, bytes_accessed=2 * width * tile * blk * 2, transcendentals=0
-        ),
-        name=f"store_{slot}_{part}",
-    )(*operands)
-
-
 def body(env_left, isometry, sing_vals, kept, twosite_sector, mpo_row, mpo_op, op_table):
     my_index = lax.axis_index("sec")
     devices = lax.axis_size("sec")
@@ -241,8 +218,6 @@
     )
     holder = where_held // per_dev
     isom = lax.all_to_all(take_blocks(isometry[0, 0], send), "sec", 0, 0, tiled=True)
-    late_env, _ = lax.optimization_barrier((env_left[0, per_dev - 2 :], isom))
-    lower = passed_along(late_env, "sec", 1)
 
     scalars = (
         holder,
@@ -255,7 +230,7 @@
     s_row = sing_vals[0][:, None, :]
     order = [(2, 0, 2), (2, 1, 2)]
     order += [(slot, 0, 1) for slot in list(range(3, per_dev)) + [1, 0]]
-    env_right = handoff = None
+    env_right = handoff = lower = None
     waiting = []
     for step, (slot, part, parts) in enumerate(order):
         below = [
@@ -279,9 +254,13 @@
         )
         env_right, hand = results[:2]
         handoff = results[2] if arrived[0] else handoff
+        if step == 2:
+            late_env, _ = lax.optimization_barrier((env_left[0, per_dev - 2 :], hand))
+            lower = passed_along(late_env, "sec", 1)
         waiting.append(((slot, part), passed_along(hand, "seg", 1)))
     for (slot, part), piece in waiting:
-        handoff = store_call(slot, part, piece, handoff, per_dev)
+        start = (0, slot, 0, part * piece.shape[1], 0)
+        handoff = lax.dynamic_update_slice(handoff, piece[None, None], start)
     return env_right, handoff
 
 

time: 349 us -> 208 us (0.60)
  Pallas kernels: 291 us -> 81 us
  waiting for transfers between devices: 6.52 us -> 71 us
  starting transfers between devices: 26.1 us -> 34.2 us
    pallas_call x8, Pallas kernels: 219 us -> 78.8 us  [sector_call(): pl.pallas_call(functools.partial(sector_kernel, slot, part * tile, stored...]
    pallas_call x2 -> x0, Pallas kernels: 69.7 us -> none  [store_call(): pl.pallas_call(functools.partial(store_kernel, (slot, part)), in_specs=[a...]
    ppermute x9, waiting for transfers between devices: 0.02 us -> 64.5 us  [passed_along(): return lax.ppermute(block, axis, route)]
    ppermute x9, starting transfers between devices: 21.9 us -> 30 us  [passed_along(): return lax.ppermute(block, axis, route)]
    unnamed x23 -> x19, local copies, waits for them, and re-layouts: 11.8 us -> 9.71 us
  transfers between devices with their start and end apart: 10 -> 10, of which waited for: 1 -> 8; matrix products, arithmetic and copies ran while one was open for 3% -> 5% of each run, Pallas kernels for 71% -> 34%
where the time goes in v2:
time: 208 us; the launch traced here: 207 us
  Pallas kernels  81 us (39%)
  waiting for transfers between devices  71 us (34%)
  starting transfers between devices  34.2 us (16%)
  local copies, waits for them, and re-layouts  17.5 us (8%)
  other arithmetic  2.75 us (1%)
    pallas_call x8, Pallas kernels, sector_call(): pl.pallas_call(functools.partial(sector_kernel, slot, part * tile, stored...  78.8 us
    ppermute x9, waiting for transfers between devices, passed_along(): return lax.ppermute(block, axis, route)  64.5 us
    ppermute x9, starting transfers between devices, passed_along(): return lax.ppermute(block, axis, route)  30 us
    unnamed x19, local copies, waits for them, and re-layouts  9.71 us
    all_to_all x1, waiting for transfers between devices, body(): lax.all_to_all(take_blocks(isometry[0, 0], send), 'sec', 0, 0, tiled=True)  6.52 us
    all_to_all x1, starting transfers between devices, body(): lax.all_to_all(take_blocks(isometry[0, 0], send), 'sec', 0, 0, tiled=True)  4.25 us
  transfers between devices with their start and end apart: 10, of which 8 were waited for; matrix products, arithmetic and copies ran while one was open for 5% of the time, Pallas kernels for 34%

profile of v2, /device:TPU:10, one launch (start us, length us, event | category | flops | bytes accessed | tf_op | source)
XLA Modules:
  0.0 207.3 jit_solution(14663870399571999415)
XLA Ops:
  0.6 0.7 bitcast_select_fusion
  1.4 0.6 select_reduce_fusion.index_ref
  2.0 2.2 %take_blocks.1 = bf16[8,4,128,128]{3,2,1,0:T(8,128)(2,1)} custom-call(s32[8]{0:T(128)} %select_reduce_fusion.index_ref, bf16[7,4,128,128]{3,2,1,0:T(8,128)(2,1)} %bitcast.15), custom_call_target="tpu_custom_call" | custom-call | tf_op jit(solution)/shard_map/take_blocks/pallas_call | solution.py:28
  4.2 4.3 %all-to-all-start = ((bf16[8,4,128,128]{3,2,1,0:T(8,128)(2,1)}), bf16[8,4,128,128]{3,2,1,0:T(8,128)(2,1)S(1)}, u32[]{:S(2)}, u32[]{:S(2)}) async-start(bf16[8,4,128,128]{3,2,1,0:T(8,128)(2,1)} %take_blocks.1), calls=%async_computation | async-start | bytes 2097152 | tf_op jit(solution)/shard_map/all_to_all | solution.py:220
  8.5 0.8 copy.38
  9.3 0.6 reshape.49.table
  9.9 0.8 copy.36
  10.7 0.7 reshape.47.row
  11.3 0.8 copy.37
  12.1 0.7 reshape.48.op
  12.8 1.7 copy.41.s_col
  14.5 0.8 select_reduce_fusion.1
  15.3 0.5 and_select_fusion.holder
  15.9 6.5 %all-to-all-done.iso = bf16[8,4,128,128]{3,2,1,0:T(8,128)(2,1)S(1)} async-done(((bf16[8,4,128,128]{3,2,1,0:T(8,128)(2,1)}), bf16[8,4,128,128]{3,2,1,0:T(8,128)(2,1)S(1)}, u32[]{:S(2)}, u32[]{:S(2)}) %all-to-all-start) | async-done | bytes 1048608 | tf_op jit(solution)/shard_map/all_to_all | solution.py:220
  22.4 0.0 copy-start
  22.4 1.0 copy-done
  23.4 7.6 %sector_2_0.1 = (bf16[1,7,34,128,128]{4,3,2,1,0:T(8,128)(2,1)}, bf16[34,64,128]{2,1,0:T(8,128)(2,1)}) custom-call(s32[7]{0:T(128)} %and_select_fusion.holder, s32[7]{0:T(128)} %bitcast.25, s32[102]{0:T(128)} %reshape.47.row, s32[102]{0:T(128)} %reshape.48.op, f32[96]{0:T(128)} %reshape.49.table, bf16[1,7,34,128,128]{4,3,2,1,0:T(8,128)(2,1)} %e0.15, ...), custom_call_target="tpu_custom_call" | custom-call | flops 71303168 | bytes 278528 | tf_op jit(solution)/shard_map/sector_2_0/pallas_call | solution.py:168
  31.0 3.5 %collective-permute-start = (bf16[34,64,128]{2,1,0:T(8,128)(2,1)}, bf16[34,64,128]{2,1,0:T(8,128)(2,1)S(1)}, u32[]{:S(2)}, u32[]{:S(2)}) collective-permute-start(bf16[34,64,128]{2,1,0:T(8,128)(2,1)} %get-tuple-element.25), channel_id=1, source_target_pairs={{0,8},{8,16},{16,24},{1,9},{9,17},{17,25},{2,10},{10,18},{18,26},{... | collective-permute-start | bytes 1671176 | tf_op jit(solution)/shard_map/ppermute | solution.py:18
  34.5 7.7 %sector_2_1.1 = (bf16[1,7,34,128,128]{4,3,2,1,0:T(8,128)(2,1)}, bf16[34,64,128]{2,1,0:T(8,128)(2,1)}) custom-call(s32[7]{0:T(128)} %and_select_fusion.holder, s32[7]{0:T(128)} %bitcast.26, s32[102]{0:T(128)} %reshape.47.row, s32[102]{0:T(128)} %reshape.48.op, f32[96]{0:T(128)} %reshape.49.table, ...), custom_call_target="tpu_custom_call", output_to_operand_aliasing={{0}: (11, {})} | custom-call | flops 71303168 | bytes 278528 | tf_op jit(solution)/shard_map/sector_2_1/pallas_call | solution.py:168
  42.2 3.5 %collective-permute-start.2 = (bf16[34,64,128]{2,1,0:T(8,128)(2,1)}, bf16[34,64,128]{2,1,0:T(8,128)(2,1)S(1)}, u32[]{:S(2)}, u32[]{:S(2)}) collective-permute-start(bf16[34,64,128]{2,1,0:T(8,128)(2,1)} %get-tuple-element.30), channel_id=1, source_target_pairs={{0,8},{8,16},{16,24},{1,9},{9,17},{17,25},{2,10},{10,18},{18,26},{... | collective-permute-start | bytes 1671176 | tf_op jit(solution)/shard_map/ppermute | solution.py:18
  45.7 2.9 %collective-permute-done.rest_0_ = bf16[34,64,128]{2,1,0:T(8,128)(2,1)S(1)} collective-permute-done((bf16[34,64,128]{2,1,0:T(8,128)(2,1)}, bf16[34,64,128]{2,1,0:T(8,128)(2,1)S(1)}, u32[]{:S(2)}, u32[]{:S(2)}) %collective-permute-start) | collective-permute-done | bytes 557088 | tf_op jit(solution)/shard_map/ppermute | solution.py:18
  48.6 0.0 copy-start.7
  48.6 0.8 copy-done.7
  49.4 10.5 %sector_3_0.1 = (bf16[1,7,34,128,128]{4,3,2,1,0:T(8,128)(2,1)}, bf16[34,128,128]{2,1,0:T(8,128)(2,1)}, bf16[1,7,34,128,128]{4,3,2,1,0:T(8,128)(2,1)}) custom-call(s32[7]{0:T(128)} %and_select_fusion.holder, s32[7]{0:T(128)} %bitcast.27, s32[102]{0:T(128)} %reshape.47.row, s32[102]{0:T(128)} %reshape.48.op, ...), custom_call_target="tpu_custom_call", output_to_operand_aliasing={{0}: (12, {})} | custom-call | flops 142606336 | bytes 557056 | tf_op jit(solution)/shard_map/sector_3_0/pallas_call | solution.py:168
  59.9 3.5 %collective-permute-start.4 = (bf16[34,128,128]{2,1,0:T(8,128)(2,1)}, bf16[34,128,128]{2,1,0:T(8,128)(2,1)S(1)}, u32[]{:S(2)}, u32[]{:S(2)}) collective-permute-start(bf16[34,128,128]{2,1,0:T(8,128)(2,1)} %get-tuple-element.28), channel_id=1, source_target_pairs={{0,8},{8,16},{16,24},{1,9},{9,17},{17,25},{2,10},{10,18},{18,26},{... | collective-permute-start | bytes 3342344 | tf_op jit(solution)/shard_map/ppermute | solution.py:18
  63.4 1.9 slice_bitcast_fusion
  65.3 1.9 collective-permute-start.1
  67.2 0.0 collective-permute-done.2.rest_0_
  67.2 0.0 copy-start.6
  67.2 0.8 copy-done.6
  68.0 10.4 %sector_4_0.1 = (bf16[1,7,34,128,128]{4,3,2,1,0:T(8,128)(2,1)}, bf16[34,128,128]{2,1,0:T(8,128)(2,1)}, bf16[1,7,34,128,128]{4,3,2,1,0:T(8,128)(2,1)}) custom-call(s32[7]{0:T(128)} %and_select_fusion.holder, s32[7]{0:T(128)} %bitcast.28, s32[102]{0:T(128)} %reshape.47.row, s32[102]{0:T(128)} %reshape.48.op, ...), custom_call_target="tpu_custom_call", output_to_operand_aliasing={{0}: (12, {}), {2}: (13, {})} | custom-call | flops 142606336 | bytes 557056 | tf_op jit(solution)/shard_map/sector_4_0/pallas_call | solution.py:168
  78.5 3.7 %collective-permute-start.3 = (bf16[34,128,128]{2,1,0:T(8,128)(2,1)}, bf16[34,128,128]{2,1,0:T(8,128)(2,1)S(1)}, u32[]{:S(2)}, u32[]{:S(2)}) collective-permute-start(bf16[34,128,128]{2,1,0:T(8,128)(2,1)} %get-tuple-element.33), channel_id=1, source_target_pairs={{0,8},{8,16},{16,24},{1,9},{9,17},{17,25},{2,10},{10,18},{18,26},{... | collective-permute-start | bytes 3342344 | tf_op jit(solution)/shard_map/ppermute | solution.py:18
  82.2 7.3 %collective-permute-done.4.rest_0_ = bf16[34,128,128]{2,1,0:T(8,128)(2,1)S(1)} collective-permute-done((bf16[34,128,128]{2,1,0:T(8,128)(2,1)}, bf16[34,128,128]{2,1,0:T(8,128)(2,1)S(1)}, u32[]{:S(2)}, u32[]{:S(2)}) %collective-permute-start.4) | collective-permute-done | bytes 1114144 | tf_op jit(solution)/shard_map/ppermute | solution.py:18
  89.5 0.0 copy-start.3
  89.5 1.0 copy-done.3
  90.5 10.7 %sector_5_0.1 = (bf16[1,7,34,128,128]{4,3,2,1,0:T(8,128)(2,1)}, bf16[34,128,128]{2,1,0:T(8,128)(2,1)}, bf16[1,7,34,128,128]{4,3,2,1,0:T(8,128)(2,1)}) custom-call(s32[7]{0:T(128)} %and_select_fusion.holder, s32[7]{0:T(128)} %bitcast.29, s32[102]{0:T(128)} %reshape.47.row, s32[102]{0:T(128)} %reshape.48.op, ...), custom_call_target="tpu_custom_call", output_to_operand_aliasing={{0}: (12, {}), {2}: (13, {})} | custom-call | flops 142606336 | bytes 557056 | tf_op jit(solution)/shard_map/sector_5_0/pallas_call | solution.py:168
  101.2 3.5 %collective-permute-start.6 = (bf16[34,128,128]{2,1,0:T(8,128)(2,1)}, bf16[34,128,128]{2,1,0:T(8,128)(2,1)S(1)}, u32[]{:S(2)}, u32[]{:S(2)}) collective-permute-start(bf16[34,128,128]{2,1,0:T(8,128)(2,1)} %get-tuple-element.39), channel_id=1, source_target_pairs={{0,8},{8,16},{16,24},{1,9},{9,17},{17,25},{2,10},{10,18},{18,26},{... | collective-permute-start | bytes 3342344 | tf_op jit(solution)/shard_map/ppermute | solution.py:18
  104.7 8.7 %collective-permute-done.3.rest_0_ = bf16[34,128,128]{2,1,0:T(8,128)(2,1)S(1)} collective-permute-done((bf16[34,128,128]{2,1,0:T(8,128)(2,1)}, bf16[34,128,128]{2,1,0:T(8,128)(2,1)S(1)}, u32[]{:S(2)}, u32[]{:S(2)}) %collective-permute-start.3) | collective-permute-done | bytes 1114144 | tf_op jit(solution)/shard_map/ppermute | solution.py:18
  113.4 0.0 copy-start.5
  113.4 1.0 copy-done.5
  114.4 10.6 %sector_6_0.1 = (bf16[1,7,34,128,128]{4,3,2,1,0:T(8,128)(2,1)}, bf16[34,128,128]{2,1,0:T(8,128)(2,1)}, bf16[1,7,34,128,128]{4,3,2,1,0:T(8,128)(2,1)}) custom-call(s32[7]{0:T(128)} %and_select_fusion.holder, s32[7]{0:T(128)} %bitcast.30, s32[102]{0:T(128)} %reshape.47.row, s32[102]{0:T(128)} %reshape.48.op, ...), custom_call_target="tpu_custom_call", output_to_operand_aliasing={{0}: (12, {}), {2}: (13, {})} | custom-call | flops 142606336 | bytes 557056 | tf_op jit(solution)/shard_map/sector_6_0/pallas_call | solution.py:168
  125.0 3.5 %collective-permute-start.5 = (bf16[34,128,128]{2,1,0:T(8,128)(2,1)}, bf16[34,128,128]{2,1,0:T(8,128)(2,1)S(1)}, u32[]{:S(2)}, u32[]{:S(2)}) collective-permute-start(bf16[34,128,128]{2,1,0:T(8,128)(2,1)} %get-tuple-element.38), channel_id=1, source_target_pairs={{0,8},{8,16},{16,24},{1,9},{9,17},{17,25},{2,10},{10,18},{18,26},{... | collective-permute-start | bytes 3342344 | tf_op jit(solution)/shard_map/ppermute | solution.py:18
  128.5 8.7 %collective-permute-done.6.rest_0_ = bf16[34,128,128]{2,1,0:T(8,128)(2,1)S(1)} collective-permute-done((bf16[34,128,128]{2,1,0:T(8,128)(2,1)}, bf16[34,128,128]{2,1,0:T(8,128)(2,1)S(1)}, u32[]{:S(2)}, u32[]{:S(2)}) %collective-permute-start.6) | collective-permute-done | bytes 1114144 | tf_op jit(solution)/shard_map/ppermute | solution.py:18
  137.2 0.0 copy-start.4
  137.2 0.0 collective-permute-done.1.e2.e1
  137.2 0.0 copy-start.1
  137.2 1.0 copy-done.4
  138.3 0.7 copy-done.1
  139.0 10.6 %sector_1_0.1 = (bf16[1,7,34,128,128]{4,3,2,1,0:T(8,128)(2,1)}, bf16[34,128,128]{2,1,0:T(8,128)(2,1)}, bf16[1,7,34,128,128]{4,3,2,1,0:T(8,128)(2,1)}) custom-call(s32[7]{0:T(128)} %and_select_fusion.holder, s32[7]{0:T(128)} %bitcast.31, s32[102]{0:T(128)} %reshape.47.row, s32[102]{0:T(128)} %reshape.48.op, ...), custom_call_target="tpu_custom_call", output_to_operand_aliasing={{0}: (12, {}), {2}: (13, {})} | custom-call | flops 142606336 | bytes 557056 | tf_op jit(solution)/shard_map/sector_1_0/pallas_call | solution.py:168
  149.6 3.5 %collective-permute-start.7 = (bf16[34,128,128]{2,1,0:T(8,128)(2,1)}, bf16[34,128,128]{2,1,0:T(8,128)(2,1)S(1)}, u32[]{:S(2)}, u32[]{:S(2)}) collective-permute-start(bf16[34,128,128]{2,1,0:T(8,128)(2,1)} %get-tuple-element.46), channel_id=1, source_target_pairs={{0,8},{8,16},{16,24},{1,9},{9,17},{17,25},{2,10},{10,18},{18,26},{... | collective-permute-start | bytes 3342344 | tf_op jit(solution)/shard_map/ppermute | solution.py:18
  153.1 8.0 %collective-permute-done.5.rest_0_ = bf16[34,128,128]{2,1,0:T(8,128)(2,1)S(1)} collective-permute-done((bf16[34,128,128]{2,1,0:T(8,128)(2,1)}, bf16[34,128,128]{2,1,0:T(8,128)(2,1)S(1)}, u32[]{:S(2)}, u32[]{:S(2)}) %collective-permute-start.5) | collective-permute-done | bytes 1114144 | tf_op jit(solution)/shard_map/ppermute | solution.py:18
  161.1 0.0 copy-start.2
  161.1 1.0 copy-done.2
  162.2 10.6 %sector_0_0.1 = (bf16[1,7,34,128,128]{4,3,2,1,0:T(8,128)(2,1)}, bf16[34,128,128]{2,1,0:T(8,128)(2,1)}, bf16[1,7,34,128,128]{4,3,2,1,0:T(8,128)(2,1)}) custom-call(s32[7]{0:T(128)} %and_select_fusion.holder, s32[7]{0:T(128)} %bitcast.32, s32[102]{0:T(128)} %reshape.47.row, s32[102]{0:T(128)} %reshape.48.op, ...), custom_call_target="tpu_custom_call", output_to_operand_aliasing={{0}: (12, {}), {2}: (13, {})} | custom-call | flops 142606336 | bytes 557056 | tf_op jit(solution)/shard_map/sector_0_0/pallas_call | solution.py:168
  172.8 3.5 %collective-permute-start.8 = (bf16[34,128,128]{2,1,0:T(8,128)(2,1)}, bf16[34,128,128]{2,1,0:T(8,128)(2,1)S(1)}, u32[]{:S(2)}, u32[]{:S(2)}) collective-permute-start(bf16[34,128,128]{2,1,0:T(8,128)(2,1)} %get-tuple-element.47), channel_id=1, source_target_pairs={{0,8},{8,16},{16,24},{1,9},{9,17},{17,25},{2,10},{10,18},{18,26},{... | collective-permute-start | bytes 3342344 | tf_op jit(solution)/shard_map/ppermute | solution.py:18
  176.3 8.7 %collective-permute-done.7 = bf16[34,128,128]{2,1,0:T(8,128)(2,1)S(1)} collective-permute-done((bf16[34,128,128]{2,1,0:T(8,128)(2,1)}, bf16[34,128,128]{2,1,0:T(8,128)(2,1)S(1)}, u32[]{:S(2)}, u32[]{:S(2)}) %collective-permute-start.7) | collective-permute-done | bytes 1114144 | tf_op jit(solution)/shard_map/ppermute | solution.py:18
  185.0 1.1 bitcast_dynamic-update-slice_fusion.1
  186.1 20.0 %collective-permute-done.8 = bf16[34,128,128]{2,1,0:T(8,128)(2,1)S(1)} collective-permute-done((bf16[34,128,128]{2,1,0:T(8,128)(2,1)}, bf16[34,128,128]{2,1,0:T(8,128)(2,1)S(1)}, u32[]{:S(2)}, u32[]{:S(2)}) %collective-permute-start.8) | collective-permute-done | bytes 1114144 | tf_op jit(solution)/shard_map/ppermute | solution.py:18
  206.2 1.1 bitcast_dynamic-update-slice_fusion
  (1 shorter events, 0.0 us)
Async XLA Ops:
  4.2 18.2 %all-to-all-start = ((bf16[8,4,128,128]{3,2,1,0:T(8,128)(2,1)}), bf16[8,4,128,128]{3,2,1,0:T(8,128)(2,1)S(1)}, u32[]{:S(2)}, u32[]{:S(2)}) async-start(bf16[8,4,128,128]{3,2,1,0:T(8,128)(2,1)} %take_blocks.1), calls=%async_computation | async-start | bytes 2097152 | tf_op jit(solution)/shard_map/all_to_all | solution.py:220
  22.4 1.0 copy-start
  31.0 17.6 %collective-permute-start = (bf16[34,64,128]{2,1,0:T(8,128)(2,1)}, bf16[34,64,128]{2,1,0:T(8,128)(2,1)S(1)}, u32[]{:S(2)}, u32[]{:S(2)}) collective-permute-start(bf16[34,64,128]{2,1,0:T(8,128)(2,1)} %get-tuple-element.25), channel_id=1, source_target_pairs={{0,8},{8,16},{16,24},{1,9},{9,17},{17,25},{2,10},{10,18},{18,26},{... | collective-permute-start | bytes 1671176 | tf_op jit(solution)/shard_map/ppermute | solution.py:18
  42.2 25.0 %collective-permute-start.2 = (bf16[34,64,128]{2,1,0:T(8,128)(2,1)}, bf16[34,64,128]{2,1,0:T(8,128)(2,1)S(1)}, u32[]{:S(2)}, u32[]{:S(2)}) collective-permute-start(bf16[34,64,128]{2,1,0:T(8,128)(2,1)} %get-tuple-element.30), channel_id=1, source_target_pairs={{0,8},{8,16},{16,24},{1,9},{9,17},{17,25},{2,10},{10,18},{18,26},{... | collective-permute-start | bytes 1671176 | tf_op jit(solution)/shard_map/ppermute | solution.py:18
  48.6 0.8 copy-start.7
  59.9 29.6 %collective-permute-start.4 = (bf16[34,128,128]{2,1,0:T(8,128)(2,1)}, bf16[34,128,128]{2,1,0:T(8,128)(2,1)S(1)}, u32[]{:S(2)}, u32[]{:S(2)}) collective-permute-start(bf16[34,128,128]{2,1,0:T(8,128)(2,1)} %get-tuple-element.28), channel_id=1, source_target_pairs={{0,8},{8,16},{16,24},{1,9},{9,17},{17,25},{2,10},{10,18},{18,26},{... | collective-permute-start | bytes 3342344 | tf_op jit(solution)/shard_map/ppermute | solution.py:18
  65.3 72.0 %collective-permute-start.1 = (bf16[2,34,128,128]{3,2,1,0:T(8,128)(2,1)S(1)}, bf16[2,34,128,128]{3,2,1,0:T(8,128)(2,1)S(1)}, u32[]{:S(2)}, u32[]{:S(2)}) collective-permute-start(bf16[2,34,128,128]{3,2,1,0:T(8,128)(2,1)S(1)} %slice_bitcast_fusion), channel_id=1, source_target_pairs={{0,1},{1,2},{2,3},{3,4},{4,5},{5,6},{6,7},{8,9},{9,10},{10,11},{11... | collective-permute-start | bytes 6684680 | tf_op jit(solution)/shard_map/ppermute | solution.py:18
  67.2 0.8 copy-start.6
  78.5 34.9 %collective-permute-start.3 = (bf16[34,128,128]{2,1,0:T(8,128)(2,1)}, bf16[34,128,128]{2,1,0:T(8,128)(2,1)S(1)}, u32[]{:S(2)}, u32[]{:S(2)}) collective-permute-start(bf16[34,128,128]{2,1,0:T(8,128)(2,1)} %get-tuple-element.33), channel_id=1, source_target_pairs={{0,8},{8,16},{16,24},{1,9},{9,17},{17,25},{2,10},{10,18},{18,26},{... | collective-permute-start | bytes 3342344 | tf_op jit(solution)/shard_map/ppermute | solution.py:18
  89.5 1.0 copy-start.3
  101.2 36.1 %collective-permute-start.6 = (bf16[34,128,128]{2,1,0:T(8,128)(2,1)}, bf16[34,128,128]{2,1,0:T(8,128)(2,1)S(1)}, u32[]{:S(2)}, u32[]{:S(2)}) collective-permute-start(bf16[34,128,128]{2,1,0:T(8,128)(2,1)} %get-tuple-element.39), channel_id=1, source_target_pairs={{0,8},{8,16},{16,24},{1,9},{9,17},{17,25},{2,10},{10,18},{18,26},{... | collective-permute-start | bytes 3342344 | tf_op jit(solution)/shard_map/ppermute | solution.py:18
  113.4 1.0 copy-start.5
  125.0 36.1 %collective-permute-start.5 = (bf16[34,128,128]{2,1,0:T(8,128)(2,1)}, bf16[34,128,128]{2,1,0:T(8,128)(2,1)S(1)}, u32[]{:S(2)}, u32[]{:S(2)}) collective-permute-start(bf16[34,128,128]{2,1,0:T(8,128)(2,1)} %get-tuple-element.38), channel_id=1, source_target_pairs={{0,8},{8,16},{16,24},{1,9},{9,17},{17,25},{2,10},{10,18},{18,26},{... | collective-permute-start | bytes 3342344 | tf_op jit(solution)/shard_map/ppermute | solution.py:18
  137.2 1.0 copy-start.4
  137.2 1.7 copy-start.1
  149.6 35.4 %collective-permute-start.7 = (bf16[34,128,128]{2,1,0:T(8,128)(2,1)}, bf16[34,128,128]{2,1,0:T(8,128)(2,1)S(1)}, u32[]{:S(2)}, u32[]{:S(2)}) collective-permute-start(bf16[34,128,128]{2,1,0:T(8,128)(2,1)} %get-tuple-element.46), channel_id=1, source_target_pairs={{0,8},{8,16},{16,24},{1,9},{9,17},{17,25},{2,10},{10,18},{18,26},{... | collective-permute-start | bytes 3342344 | tf_op jit(solution)/shard_map/ppermute | solution.py:18
  161.1 1.0 copy-start.2
  172.8 33.3 %collective-permute-start.8 = (bf16[34,128,128]{2,1,0:T(8,128)(2,1)}, bf16[34,128,128]{2,1,0:T(8,128)(2,1)S(1)}, u32[]{:S(2)}, u32[]{:S(2)}) collective-permute-start(bf16[34,128,128]{2,1,0:T(8,128)(2,1)} %get-tuple-element.47), channel_id=1, source_target_pairs={{0,8},{8,16},{16,24},{1,9},{9,17},{17,25},{2,10},{10,18},{18,26},{... | collective-permute-start | bytes 3342344 | tf_op jit(solution)/shard_map/ppermute | solution.py:18
